TPU v7x, 256 devices: a whole 4x4x8 slice. The times are simulated.
256 devices in a mesh: shard: 64 (over z, x_lo, y), blk: 4 (over x_hi, core).
Axes of the slice: x: 4 (x_hi: 2, x_lo: 2; x = x_hi * 2 + x_lo), y: 4, z: 8, core: 2. Of those that a mesh axis runs over, the one named last changes fastest.
Arguments:
- embeddings: bfloat16 [65536, 1024], P(('shard', 'blk')), may hold values from -6 to 6
- doc_cluster: int32 [65536], P(('shard', 'blk')), may hold values from 0 to 255, as said below
- doc_valid: int32 [65536], P(('shard', 'blk')), may hold values 0 or 1
Outputs:
- max_similar: float32 [65536], P(('shard', 'blk'))
Inputs may be any that keep to these rules, and one draw needn't show every extreme that they name: `doc_cluster`: among the documents of one device at most 16 have clusters of one owner group (cluster mod 64), and at most 4 have clusters c of one owner group with one value of (c // 64) mod 4; one owner group, the same on every device, gets exactly 16 from every device, 4 for each such value.
All inputs are finite; a program needn't handle non-finite values. No bound on the sum of `doc_valid` on one device may be relied on, other than what follows from the above.
Results may differ from a plain program's by a relative error of at most 0.00036.
Values may be sent and summed in bfloat16 or wider, within the bound.
A program may use at most 64 MiB of HBM per device.

v0:
```python
import math
import jax
import jax.numpy as jnp
from jax import lax
from jax.sharding import PartitionSpec as P


def unit_rows(embeddings):
    values = embeddings.astype(jnp.float32)
    scale = lax.rsqrt(jnp.mean(values * values, axis=1, keepdims=True) + 1e-05) / math.sqrt(
        values.shape[1]
    )
    return (values * scale).astype(jnp.bfloat16)


def scores_max(rows_query, keys_query, ids_query, rows_other, keys_other, ids_other, key_block):
    query_count = rows_query.shape[0]
    block_rows = 512

    def one_block(block):
        rows_part, keys_part, ids_part = block
        best = jnp.full((rows_part.shape[0],), -1.0, jnp.float32)
        for number in range(rows_other.shape[0] // key_block):
            first = number * key_block
            rows_key = rows_other[first : first + key_block]
            keys_key = keys_other[first : first + key_block]
            ids_key = ids_other[first : first + key_block]
            similar = lax.dot_general(
                rows_part, rows_key, (((1,), (1,)), ((), ())), preferred_element_type=jnp.float32
            )
            same_group = (
                (keys_part[:, None] == keys_key[None, :])
                & (keys_part[:, None] >= 0)
                & (ids_part[:, None] != ids_key[None, :])
            )
            best = jnp.maximum(best, jnp.max(jnp.where(same_group, similar, -1.0), axis=1))
        return best

    stacked = (
        rows_query.reshape(query_count // block_rows, block_rows, -1),
        keys_query.reshape(query_count // block_rows, block_rows),
        ids_query.reshape(query_count // block_rows, block_rows),
    )
    return lax.map(one_block, stacked).reshape(query_count)


def slot_numbers(target, targets, per_target):
    one_hot = (target[:, None] == jnp.arange(targets, dtype=jnp.int32)[None, :]).astype(jnp.int32)
    ranks = jnp.sum((jnp.cumsum(one_hot, axis=0) - 1) * one_hot, axis=1)
    return target * per_target + ranks


def per_device(embeddings, doc_cluster, doc_valid):
    dev_rows, width = embeddings.shape
    shards = lax.axis_size("shard")
    blocks = lax.axis_size("blk")
    capacity = max(blocks, 4 * dev_rows // shards)
    slots = shards * capacity
    device = lax.axis_index("shard") * blocks + lax.axis_index("blk")
    doc_ids = device * dev_rows + jnp.arange(dev_rows, dtype=jnp.int32)
    owner = doc_cluster % shards
    slot_of = slot_numbers(owner, shards, capacity)
    keyed = jnp.where(doc_valid > 0, doc_cluster, -1)
    flat_rows = jnp.zeros((slots, width), jnp.bfloat16).at[slot_of].set(unit_rows(embeddings))
    flat_keys = jnp.full((slots,), -1, jnp.int32).at[slot_of].set(keyed)
    flat_ids = jnp.full((slots,), -1, jnp.int32).at[slot_of].set(doc_ids)
    send_rows = flat_rows.reshape(shards, capacity, width)
    send_keys = flat_keys.reshape(shards, capacity)
    send_ids = flat_ids.reshape(shards, capacity)
    got_rows, got_keys, got_ids = (
        lax.all_to_all(send_rows, "shard", split_axis=0, concat_axis=0, tiled=True),
        lax.all_to_all(send_keys, "shard", split_axis=0, concat_axis=0, tiled=True),
        lax.all_to_all(send_ids, "shard", split_axis=0, concat_axis=0, tiled=True),
    )
    query_rows = got_rows.reshape(slots, width)
    query_keys = got_keys.reshape(slots)
    query_ids = got_ids.reshape(slots)
    best = jnp.maximum(
        jnp.full((slots,), -1.0, jnp.float32),
        scores_max(
            query_rows,
            query_keys,
            query_ids,
            lax.all_gather(query_rows, "blk", axis=0, tiled=True),
            lax.all_gather(query_keys, "blk", axis=0, tiled=True),
            lax.all_gather(query_ids, "blk", axis=0, tiled=True),
            slots,
        ),
    )
    verdict = lax.all_to_all(
        best.reshape(shards, capacity), "shard", split_axis=0, concat_axis=0, tiled=True
    )
    return verdict.reshape(slots)[slot_of]


def solution(mesh):
    placed = (P(("shard", "blk"), None), P(("shard", "blk")), P(("shard", "blk")))
    return jax.shard_map(
        per_device, mesh=mesh, in_specs=placed, out_specs=P(("shard", "blk")), check_vma=False
    )
```

profile of v0, /device:TPU:1, one launch (start us, length us, event | category | flops | bytes accessed | tf_op | source)
XLA Modules:
  0.0 188.0 jit_solution(3267887966830044788)
XLA Ops:
  8.2 1.2 fusion.28
  9.5 2.9 %scatter_custom_fusion.2 = bf16[1024,1024]{1,0:T(8,128)(2,1)S(1)} fusion(s32[256]{0:T(256)S(1)} %get-tuple-element.80, bf16[]{:T(256)} %constant.32.clone.1, bf16[256,1024]{1,0:T(8,128)(2,1)} %param.5, f32[256]{0:T(256)S(1)} %rsqrt_multiply_fusion), kind=kCustom, calls=%fused_computation.36 | custom fusion | flops 786432 | bytes 2622466 | tf_op jit(solution)/shard_map/scatter | solution.py:64
  12.4 61.9 %all_to_all.29 = bf16[64,16,1024]{2,1,0:T(8,128)(2,1)} all-to-all(bf16[64,16,1024]{2,1,0:T(8,128)(2,1)S(1)} %bitcast.52), channel_id=1, replica_groups=mesh['shard'=64,'blk'=4] {'shard'}, dimensions={0} | all-to-all | bytes 4194304 | tf_op jit(solution)/shard_map/all_to_all | solution.py:71
  74.3 1.4 scatter_custom_fusion.1
  76.4 7.6 %all-to-all-start.1 = ((s32[64,1,16]{2,1,0:T(1,128)}), s32[64,1,16]{2,1,0:T(1,128)S(1)}, u32[]{:S(2)}, u32[]{:S(2)}) async-start(s32[64,1,16]{2,1,0:T(1,128)} %bitcast.7), calls=%async_computation.1 | async-start | bytes 65536 | tf_op jit(solution)/shard_map/all_to_all | solution.py:73
  84.1 1.4 scatter_custom_fusion
  86.2 7.2 %all-to-all-done.1 = s32[64,1,16]{2,1,0:T(1,128)S(1)} async-done(((s32[64,1,16]{2,1,0:T(1,128)}), s32[64,1,16]{2,1,0:T(1,128)S(1)}, u32[]{:S(2)}, u32[]{:S(2)}) %all-to-all-start.1) | async-done | bytes 4128 | tf_op jit(solution)/shard_map/all_to_all | solution.py:73
  93.4 4.6 %all-to-all-start = ((s32[64,1,16]{2,1,0:T(1,128)}), s32[64,1,16]{2,1,0:T(1,128)S(1)}, u32[]{:S(2)}, u32[]{:S(2)}) async-start(s32[64,1,16]{2,1,0:T(1,128)} %bitcast.6), calls=%async_computation | async-start | bytes 65536 | tf_op jit(solution)/shard_map/all_to_all | solution.py:72
  99.5 7.8 %all-to-all-done = s32[64,1,16]{2,1,0:T(1,128)S(1)} async-done(((s32[64,1,16]{2,1,0:T(1,128)}), s32[64,1,16]{2,1,0:T(1,128)S(1)}, u32[]{:S(2)}, u32[]{:S(2)}) %all-to-all-start) | async-done | bytes 4128 | tf_op jit(solution)/shard_map/all_to_all | solution.py:72
  108.1 10.9 %all_gather.10 = s32[4096]{0:T(1024)S(1)} all-gather(s32[1024]{0:T(1024)S(1)} %reshape.127), channel_id=1, replica_groups=mesh['shard'=64,'blk'=4] {'blk'}, dimensions={0}, use_global_device_ids=true | all-gather | bytes 20480 | tf_op jit(solution)/shard_map/all_gather | solution.py:86
  119.0 6.9 %all_gather.9 = s32[4096]{0:T(1024)S(1)} all-gather(s32[1024]{0:T(1024)S(1)} %reshape.126), channel_id=1, replica_groups=mesh['shard'=64,'blk'=4] {'blk'}, dimensions={0}, use_global_device_ids=true | all-gather | bytes 20480 | tf_op jit(solution)/shard_map/all_gather | solution.py:85
  125.9 14.1 %all-gather.2.cloned.1.call-done = bf16[4096,1024]{1,0:T(8,128)(2,1)} async-done(((bf16[1024,1024]{1,0:T(8,128)(2,1)}), bf16[4096,1024]{1,0:T(8,128)(2,1)}) %all-gather.2.cloned.1.call-update) | async-done | bytes 8388624 | tf_op jit(solution)/shard_map/all_gather | solution.py:84
  140.1 17.7 %while.10 = (s32[]{:T(128)}, f32[2,512]{1,0:T(2,128)S(1)}, s32[2,512]{1,0:T(2,128)S(1)}, s32[4096]{0:T(1024)S(1)}, s32[2,512]{1,0:T(2,128)S(1)}, /*index=5*/s32[...) while((s32[]{:T(128)}, f32[2,512]{1,0:T(2,128)S(1)}, ...), condition=%wide.region_12.13_spmd, body=%wide.region_7.12_spmd.sunk | while | flops 4307550720 | bytes 46288020 | solution.py:44
  140.1 3.3 %select_reduce_fusion.11 = f32[512]{0:T(512)S(1)} fusion(bf16[4096,1024]{1,0:T(8,128)(2,1)} %get-tuple-element.178, s32[1024]{0:T(1024)S(1)} %get-tuple-element.149, s32[1024]{0:T(1024)S(1)} %get-tuple-element.150, pred[512]{0:T(512)(128)(4,1)S(1)} %broadcast_compare_fusion.2, s32[512]{0:T(512)S(1)} %bitcast.61, s32[512]{0:T(512)S(1)} %bitcast.56, ...), kind=kOutput, calls=%fused_computation.13.clone.1 | convolution fusion | flops 1076887040 | bytes 3161088 | tf_op jit(solution)/shard_map/while/body/eval_jaxpr/dot_general | solution.py:28
  144.1 1.6 select_reduce_fusion.10
  145.7 1.6 select_reduce_fusion.9
  147.3 1.6 select_reduce_fusion.8
  149.0 3.3 %select_reduce_fusion.11 = f32[512]{0:T(512)S(1)} fusion(bf16[4096,1024]{1,0:T(8,128)(2,1)} %get-tuple-element.178, s32[1024]{0:T(1024)S(1)} %get-tuple-element.149, s32[1024]{0:T(1024)S(1)} %get-tuple-element.150, pred[512]{0:T(512)(128)(4,1)S(1)} %broadcast_compare_fusion.2, s32[512]{0:T(512)S(1)} %bitcast.61, s32[512]{0:T(512)S(1)} %bitcast.56, ...), kind=kOutput, calls=%fused_computation.13.clone.1 | convolution fusion | flops 1076887040 | bytes 3161088 | tf_op jit(solution)/shard_map/while/body/eval_jaxpr/dot_general | solution.py:28
  153.0 1.6 select_reduce_fusion.10
  154.6 1.6 select_reduce_fusion.9
  156.1 1.6 select_reduce_fusion.8
  158.5 10.1 %all-to-all-start.3 = ((f32[64,1,16]{2,1,0:T(1,128)}), f32[64,1,16]{2,1,0:T(1,128)S(1)}, u32[]{:S(2)}, u32[]{:S(2)}) async-start(f32[64,1,16]{2,1,0:T(1,128)} %bitcast.11), calls=%async_computation.3 | async-start | bytes 65536 | tf_op jit(solution)/shard_map/all_to_all | solution.py:90
  168.6 9.3 %all-to-all-done.3 = f32[64,1,16]{2,1,0:T(1,128)S(1)} async-done(((f32[64,1,16]{2,1,0:T(1,128)}), f32[64,1,16]{2,1,0:T(1,128)S(1)}, u32[]{:S(2)}, u32[]{:S(2)}) %all-to-all-start.3) | async-done | bytes 4128 | tf_op jit(solution)/shard_map/all_to_all | solution.py:90
  179.3 1.9 %gather_fusion = f32[256]{0:T(256)} fusion(f32[1024]{0:T(1024)S(1)} %reshape.130, s32[1024]{0:T(1024)S(1)} %pad_clamp_fusion), kind=kCustom, calls=%fused_computation | custom fusion | bytes 3072 | tf_op jit(solution)/shard_map/gather | solution.py:93
  (43 shorter events, 9.0 us)
Async XLA Ops:
  6.5 133.5 %all-gather.2.cloned.1.call-start = ((), (), s32[]{:S(2)}) async-start(), calls=%async_computation.4 | async-start | bytes 10485760 | tf_op jit(solution)/shard_map/all_gather | solution.py:84
  74.3 65.7 %copy-start = (bf16[64,16,1024]{2,1,0:T(8,128)(2,1)S(1)}, bf16[64,16,1024]{2,1,0:T(8,128)(2,1)}, u32[]{:S(2)}) copy-start(bf16[64,16,1024]{2,1,0:T(8,128)(2,1)} %all_to_all.29) | copy-start | bytes 6291460
  76.4 16.9 %all-to-all-start.1 = ((s32[64,1,16]{2,1,0:T(1,128)}), s32[64,1,16]{2,1,0:T(1,128)S(1)}, u32[]{:S(2)}, u32[]{:S(2)}) async-start(s32[64,1,16]{2,1,0:T(1,128)} %bitcast.7), calls=%async_computation.1 | async-start | bytes 65536 | tf_op jit(solution)/shard_map/all_to_all | solution.py:73
  93.4 13.9 %all-to-all-start = ((s32[64,1,16]{2,1,0:T(1,128)}), s32[64,1,16]{2,1,0:T(1,128)S(1)}, u32[]{:S(2)}, u32[]{:S(2)}) async-start(s32[64,1,16]{2,1,0:T(1,128)} %bitcast.6), calls=%async_computation | async-start | bytes 65536 | tf_op jit(solution)/shard_map/all_to_all | solution.py:72
  140.1 4.0 %copy-start.1 = (bf16[4096,1024]{1,0:T(8,128)(2,1)S(1)}, bf16[4096,1024]{1,0:T(8,128)(2,1)}, u32[]{:S(2)}) copy-start(bf16[4096,1024]{1,0:T(8,128)(2,1)} %get-tuple-element.178) | copy-start | bytes 25165828 | tf_op jit(solution)/shard_map/while
  149.0 4.0 %copy-start.1 = (bf16[4096,1024]{1,0:T(8,128)(2,1)S(1)}, bf16[4096,1024]{1,0:T(8,128)(2,1)}, u32[]{:S(2)}) copy-start(bf16[4096,1024]{1,0:T(8,128)(2,1)} %get-tuple-element.178) | copy-start | bytes 25165828 | tf_op jit(solution)/shard_map/while
  158.5 19.5 %all-to-all-start.3 = ((f32[64,1,16]{2,1,0:T(1,128)}), f32[64,1,16]{2,1,0:T(1,128)S(1)}, u32[]{:S(2)}, u32[]{:S(2)}) async-start(f32[64,1,16]{2,1,0:T(1,128)} %bitcast.11), calls=%async_computation.3 | async-start | bytes 65536 | tf_op jit(solution)/shard_map/all_to_all | solution.py:90
Sparse Core Ops, SparseCore 0:
  74.5 65.5 all-gather.1
where the time goes:
time: 188 us
  blocking collectives  79.7 us (42%)
  waiting for transfers between devices  38.4 us (20%)
  starting transfers between devices  22.3 us (12%)
  matrix products  16.1 us (9%)
  between operations  13.5 us (7%)
  local copies, waits for them, and re-layouts  9.96 us (5%)
  other arithmetic  7.88 us (4%)
    all_to_all x1, blocking collectives, per_device(): lax.all_to_all(send_rows, 'shard', split_axis=0, concat_axis=0, tiled=True)  61.9 us
    dot_general x8, matrix products, one_block(): lax.dot_general(rows_part, rows_key, (((1,), (1,)), ((), ())), preferred_...  16.1 us
    all_gather x1, waiting for transfers between devices, per_device(): lax.all_gather(query_rows, 'blk', axis=0, tiled=True)  14.1 us
    all_gather x1, blocking collectives, per_device(): lax.all_gather(query_ids, 'blk', axis=0, tiled=True)  10.9 us
    all_to_all x1, starting transfers between devices, per_device(): lax.all_to_all(best.reshape(shards, capacity), 'shard', split_axis=0, con...  10.1 us
    all_to_all x1, waiting for transfers between devices, per_device(): lax.all_to_all(best.reshape(shards, capacity), 'shard', split_axis=0, con...  9.32 us
    all_to_all x1, waiting for transfers between devices, per_device(): lax.all_to_all(send_keys, 'shard', split_axis=0, concat_axis=0, tiled=True)  7.76 us
    all_to_all x1, starting transfers between devices, per_device(): lax.all_to_all(send_ids, 'shard', split_axis=0, concat_axis=0, tiled=True)  7.63 us
  transfers between devices with their start and end apart: 4, of which 4 were waited for; matrix products, arithmetic and copies ran while one was open for 3% of the time, Pallas kernels for 0%

commit v1 on v0

--- a/solution.py
+++ b/solution.py
@@ -81,7 +81,9 @@
             query_rows,
             query_keys,
             query_ids,
-            lax.all_gather(query_rows, "blk", axis=0, tiled=True),
+            jnp.concatenate(
+                lax.all_to_all(jnp.stack([query_rows] * lax.axis_size("blk")), "blk", 0, 0), axis=0
+            ),
             lax.all_gather(query_keys, "blk", axis=0, tiled=True),
             lax.all_gather(query_ids, "blk", axis=0, tiled=True),
             slots,

time: 188 us -> 256 us (1.36)
  blocking collectives: 79.7 us -> 152 us
  waiting for transfers between devices: 38.4 us -> 20.6 us
  between operations: 13.5 us -> 0.12 us
  starting transfers between devices: 22.3 us -> 35.4 us
  matrix products: 16.1 us -> 25.2 us
  local copies, waits for them, and re-layouts: 9.96 us -> 12.8 us
    all_gather x1, blocking collectives: 10.9 us -> 93.3 us  [per_device(): lax.all_gather(query_ids, 'blk', axis=0, tiled=True)]
    all_gather x1 -> x0, waiting for transfers between devices: 14.1 us -> none  [per_device(): lax.all_gather(query_rows, 'blk', axis=0, tiled=True)]
    all_to_all x0 -> x1, starting transfers between devices: none -> 10.6 us  [per_device(): lax.all_to_all(jnp.stack([query_rows] * lax.axis_size('blk')), 'blk', 0, 0)]
    all_to_all x1, blocking collectives: 61.9 us -> 51.7 us  [per_device(): lax.all_to_all(send_rows, 'shard', split_axis=0, concat_axis=0, tiled=True)]
    dot_general x8, matrix products: 16.1 us -> 25.2 us  [one_block(): lax.dot_general(rows_part, rows_key, (((1,), (1,)), ((), ())), preferred_...]
    all_to_all x1, starting transfers between devices: 7.63 us -> 13.6 us  [per_device(): lax.all_to_all(send_ids, 'shard', split_axis=0, concat_axis=0, tiled=True)]
    another operation x1 -> x2, local copies, waits for them, and re-layouts: 0.01 us -> 4.32 us  [the longest x1 4.31 us: per_device(): jnp.stack([query_rows] * lax.axis_size('blk'))]
    all_to_all x1, starting transfers between devices: 10.1 us -> 6.52 us  [per_device(): lax.all_to_all(best.reshape(shards, capacity), 'shard', split_axis=0, con...]
  transfers between devices with their start and end apart: 4 -> 4, of which waited for: 4 -> 3; matrix products, arithmetic and copies ran while one was open for 3% -> 3% of each run, Pallas kernels for 0% -> 0%
where the time goes in v1:
time: 256 us; the launch traced here: 255 us
  blocking collectives  152 us (59%)
  starting transfers between devices  35.4 us (14%)
  matrix products  25.2 us (10%)
  waiting for transfers between devices  20.6 us (8%)
  local copies, waits for them, and re-layouts  12.8 us (5%)
  other arithmetic  8.59 us (3%)
    all_gather x1, blocking collectives, per_device(): lax.all_gather(query_ids, 'blk', axis=0, tiled=True)  93.3 us
    all_to_all x1, blocking collectives, per_device(): lax.all_to_all(send_rows, 'shard', split_axis=0, concat_axis=0, tiled=True)  51.7 us
    dot_general x8, matrix products, one_block(): lax.dot_general(rows_part, rows_key, (((1,), (1,)), ((), ())), preferred_...  25.2 us
    all_to_all x1, starting transfers between devices, per_device(): lax.all_to_all(send_ids, 'shard', split_axis=0, concat_axis=0, tiled=True)  13.6 us
    all_to_all x1, starting transfers between devices, per_device(): lax.all_to_all(jnp.stack([query_rows] * lax.axis_size('blk')), 'blk', 0, 0)  10.6 us
    all_to_all x1, waiting for transfers between devices, per_device(): lax.all_to_all(best.reshape(shards, capacity), 'shard', split_axis=0, con...  9.31 us
    all_gather x1, blocking collectives, per_device(): lax.all_gather(query_keys, 'blk', axis=0, tiled=True)  6.85 us
    all_to_all x1, starting transfers between devices, per_device(): lax.all_to_all(best.reshape(shards, capacity), 'shard', split_axis=0, con...  6.52 us
  transfers between devices with their start and end apart: 4, of which 3 were waited for; matrix products, arithmetic and copies ran while one was open for 3% of the time, Pallas kernels for 0%

profile of v1, /device:TPU:1, one launch (start us, length us, event | category | flops | bytes accessed | tf_op | source)
XLA Modules:
  0.0 254.7 jit_solution(6590088186813413441)
XLA Ops:
  1.7 1.4 scatter_custom_fusion.1
  3.8 13.6 %all-to-all-start.1 = ((s32[64,1,16]{2,1,0:T(1,128)}), s32[64,1,16]{2,1,0:T(1,128)S(1)}, u32[]{:S(2)}, u32[]{:S(2)}) async-start(s32[64,1,16]{2,1,0:T(1,128)} %bitcast.7), calls=%async_computation.1 | async-start | bytes 65536 | tf_op jit(solution)/shard_map/all_to_all | solution.py:73
  18.6 1.4 scatter_custom_fusion
  20.7 6.0 %all-to-all-done.1 = s32[64,1,16]{2,1,0:T(1,128)S(1)} async-done(((s32[64,1,16]{2,1,0:T(1,128)}), s32[64,1,16]{2,1,0:T(1,128)S(1)}, u32[]{:S(2)}, u32[]{:S(2)}) %all-to-all-start.1) | async-done | bytes 4128 | tf_op jit(solution)/shard_map/all_to_all | solution.py:73
  26.6 4.7 %all-to-all-start = ((s32[64,1,16]{2,1,0:T(1,128)}), s32[64,1,16]{2,1,0:T(1,128)S(1)}, u32[]{:S(2)}, u32[]{:S(2)}) async-start(s32[64,1,16]{2,1,0:T(1,128)} %bitcast.6), calls=%async_computation | async-start | bytes 65536 | tf_op jit(solution)/shard_map/all_to_all | solution.py:72
  31.4 3.8 %scatter_custom_fusion.2 = bf16[1024,1024]{1,0:T(8,128)(2,1)} fusion(s32[256]{0:T(256)S(1)} %get-tuple-element.80, bf16[]{:T(256)} %constant.32.clone.1, bf16[256,1024]{1,0:T(8,128)(2,1)} %param.5, f32[256]{0:T(256)S(1)} %rsqrt_multiply_fusion), kind=kCustom, calls=%fused_computation.36 | custom fusion | flops 786432 | bytes 2622466 | tf_op jit(solution)/shard_map/scatter | solution.py:64
  35.2 5.4 %all-to-all-done = s32[64,1,16]{2,1,0:T(1,128)S(1)} async-done(((s32[64,1,16]{2,1,0:T(1,128)}), s32[64,1,16]{2,1,0:T(1,128)S(1)}, u32[]{:S(2)}, u32[]{:S(2)}) %all-to-all-start) | async-done | bytes 4128 | tf_op jit(solution)/shard_map/all_to_all | solution.py:72
  40.5 51.7 %all_to_all.34 = bf16[64,16,1024]{2,1,0:T(8,128)(2,1)S(1)} all-to-all(bf16[64,16,1024]{2,1,0:T(8,128)(2,1)} %bitcast.53), channel_id=1, replica_groups=mesh['shard'=64,'blk'=4] {'shard'}, dimensions={0} | all-to-all | bytes 4194304 | tf_op jit(solution)/shard_map/all_to_all | solution.py:71
  92.3 4.3 %stack.3 = bf16[4,1024,1024]{2,1,0:T(8,128)(2,1)} broadcast(bf16[1024,1024]{1,0:T(8,128)(2,1)S(1)} %bitcast.51), dimensions={1,2} | broadcast | bytes 10485760 | tf_op jit(solution)/shard_map/stack | solution.py:85
  96.6 10.6 %all-to-all-start.3 = ((bf16[4,1024,1024]{2,1,0:T(8,128)(2,1)}), bf16[4,1024,1024]{2,1,0:T(8,128)(2,1)}, u32[]{:S(2)}, u32[]{:S(2)}) async-start(bf16[4,1024,1024]{2,1,0:T(8,128)(2,1)} %stack.3), calls=%async_computation.3 | async-start | bytes 16777216 | tf_op jit(solution)/shard_map/all_to_all | solution.py:85
  109.3 93.3 %all_gather.7 = s32[4096]{0:T(1024)S(1)} all-gather(s32[1024]{0:T(1024)S(1)} %reshape.129), channel_id=1, replica_groups=mesh['shard'=64,'blk'=4] {'blk'}, dimensions={0}, use_global_device_ids=true | all-gather | bytes 20480 | tf_op jit(solution)/shard_map/all_gather | solution.py:88
  202.6 6.9 %all_gather.6 = s32[4096]{0:T(1024)S(1)} all-gather(s32[1024]{0:T(1024)S(1)} %reshape.128), channel_id=1, replica_groups=mesh['shard'=64,'blk'=4] {'blk'}, dimensions={0}, use_global_device_ids=true | all-gather | bytes 20480 | tf_op jit(solution)/shard_map/all_gather | solution.py:87
  209.4 25.5 %while.10 = (s32[]{:T(128)}, f32[2,512]{1,0:T(2,128)S(1)}, s32[2,512]{1,0:T(2,128)S(1)}, s32[4096]{0:T(1024)S(1)}, s32[2,512]{1,0:T(2,128)S(1)}, /*index=5*/s32[...) while((s32[]{:T(128)}, f32[2,512]{1,0:T(2,128)S(1)}, ...), condition=%wide.region_12.13_spmd, body=%wide.region_7.12_spmd.sunk | while | flops 4307550720 | bytes 12735085 | solution.py:44
  209.5 3.2 %select_reduce_fusion.11 = f32[512]{0:T(512)S(1)} fusion(bf16[4096,1024]{1,0:T(8,128)(2,1)} %get-tuple-element.178, s32[1024]{0:T(1024)S(1)} %get-tuple-element.149, s32[1024]{0:T(1024)S(1)} %get-tuple-element.150, pred[512]{0:T(512)(128)(4,1)S(1)} %broadcast_compare_fusion.2, s32[512]{0:T(512)S(1)} %bitcast.62, s32[512]{0:T(512)S(1)} %bitcast.57, ...), kind=kOutput, calls=%fused_computation.13.clone.1 | convolution fusion | flops 1076887040 | bytes 3161088 | tf_op jit(solution)/shard_map/while/body/eval_jaxpr/dot_general | solution.py:28
  212.6 3.1 %select_reduce_fusion.10 = f32[512]{0:T(512)S(1)} fusion(bf16[4096,1024]{1,0:T(8,128)(2,1)} %get-tuple-element.178, s32[1024]{0:T(1024)S(1)} %get-tuple-element.147, s32[1024]{0:T(1024)S(1)} %get-tuple-element.148, pred[512]{0:T(512)(128)(4,1)S(1)} %broadcast_compare_fusion.2, s32[512]{0:T(512)S(1)} %bitcast.63, s32[512]{0:T(512)S(1)} %bitcast.58, ...), kind=kOutput, calls=%fused_computation.10.clone.1 | convolution fusion | flops 1076887040 | bytes 3161088 | tf_op jit(solution)/shard_map/while/body/eval_jaxpr/dot_general | solution.py:28
  215.8 3.2 %select_reduce_fusion.9 = f32[512]{0:T(512)S(1)} fusion(bf16[4096,1024]{1,0:T(8,128)(2,1)} %get-tuple-element.178, s32[1024]{0:T(1024)S(1)} %get-tuple-element.145, s32[1024]{0:T(1024)S(1)} %get-tuple-element.146, pred[512]{0:T(512)(128)(4,1)S(1)} %broadcast_compare_fusion.2, s32[512]{0:T(512)S(1)} %bitcast.64, s32[512]{0:T(512)S(1)} %bitcast.59, ...), kind=kOutput, calls=%fused_computation.7.clone.1 | convolution fusion | flops 1076887040 | bytes 3161088 | tf_op jit(solution)/shard_map/while/body/eval_jaxpr/dot_general | solution.py:28
  219.0 3.2 %select_reduce_fusion.8 = f32[512]{0:T(512)S(1)} fusion(bf16[4096,1024]{1,0:T(8,128)(2,1)} %get-tuple-element.178, s32[1024]{0:T(1024)S(1)} %get-tuple-element.141, s32[1024]{0:T(1024)S(1)} %get-tuple-element.142, pred[512]{0:T(512)(128)(4,1)S(1)} %broadcast_compare_fusion.2, s32[512]{0:T(512)S(1)} %bitcast.65, s32[512]{0:T(512)S(1)} %bitcast.60, ...), kind=kOutput, calls=%fused_computation.4.clone.1 | convolution fusion | flops 1076887040 | bytes 3161088 | tf_op jit(solution)/shard_map/while/body/eval_jaxpr/dot_general | solution.py:28
  222.2 3.2 %select_reduce_fusion.11 = f32[512]{0:T(512)S(1)} fusion(bf16[4096,1024]{1,0:T(8,128)(2,1)} %get-tuple-element.178, s32[1024]{0:T(1024)S(1)} %get-tuple-element.149, s32[1024]{0:T(1024)S(1)} %get-tuple-element.150, pred[512]{0:T(512)(128)(4,1)S(1)} %broadcast_compare_fusion.2, s32[512]{0:T(512)S(1)} %bitcast.62, s32[512]{0:T(512)S(1)} %bitcast.57, ...), kind=kOutput, calls=%fused_computation.13.clone.1 | convolution fusion | flops 1076887040 | bytes 3161088 | tf_op jit(solution)/shard_map/while/body/eval_jaxpr/dot_general | solution.py:28
  225.4 3.2 %select_reduce_fusion.10 = f32[512]{0:T(512)S(1)} fusion(bf16[4096,1024]{1,0:T(8,128)(2,1)} %get-tuple-element.178, s32[1024]{0:T(1024)S(1)} %get-tuple-element.147, s32[1024]{0:T(1024)S(1)} %get-tuple-element.148, pred[512]{0:T(512)(128)(4,1)S(1)} %broadcast_compare_fusion.2, s32[512]{0:T(512)S(1)} %bitcast.63, s32[512]{0:T(512)S(1)} %bitcast.58, ...), kind=kOutput, calls=%fused_computation.10.clone.1 | convolution fusion | flops 1076887040 | bytes 3161088 | tf_op jit(solution)/shard_map/while/body/eval_jaxpr/dot_general | solution.py:28
  228.5 3.2 %select_reduce_fusion.9 = f32[512]{0:T(512)S(1)} fusion(bf16[4096,1024]{1,0:T(8,128)(2,1)} %get-tuple-element.178, s32[1024]{0:T(1024)S(1)} %get-tuple-element.145, s32[1024]{0:T(1024)S(1)} %get-tuple-element.146, pred[512]{0:T(512)(128)(4,1)S(1)} %broadcast_compare_fusion.2, s32[512]{0:T(512)S(1)} %bitcast.64, s32[512]{0:T(512)S(1)} %bitcast.59, ...), kind=kOutput, calls=%fused_computation.7.clone.1 | convolution fusion | flops 1076887040 | bytes 3161088 | tf_op jit(solution)/shard_map/while/body/eval_jaxpr/dot_general | solution.py:28
  231.7 3.2 %select_reduce_fusion.8 = f32[512]{0:T(512)S(1)} fusion(bf16[4096,1024]{1,0:T(8,128)(2,1)} %get-tuple-element.178, s32[1024]{0:T(1024)S(1)} %get-tuple-element.141, s32[1024]{0:T(1024)S(1)} %get-tuple-element.142, pred[512]{0:T(512)(128)(4,1)S(1)} %broadcast_compare_fusion.2, s32[512]{0:T(512)S(1)} %bitcast.65, s32[512]{0:T(512)S(1)} %bitcast.60, ...), kind=kOutput, calls=%fused_computation.4.clone.1 | convolution fusion | flops 1076887040 | bytes 3161088 | tf_op jit(solution)/shard_map/while/body/eval_jaxpr/dot_general | solution.py:28
  235.6 6.5 %all-to-all-start.4 = ((f32[64,1,16]{2,1,0:T(1,128)}), f32[64,1,16]{2,1,0:T(1,128)S(1)}, u32[]{:S(2)}, u32[]{:S(2)}) async-start(f32[64,1,16]{2,1,0:T(1,128)} %bitcast.12), calls=%async_computation.4 | async-start | bytes 65536 | tf_op jit(solution)/shard_map/all_to_all | solution.py:92
  242.2 9.3 %all-to-all-done.4 = f32[64,1,16]{2,1,0:T(1,128)S(1)} async-done(((f32[64,1,16]{2,1,0:T(1,128)}), f32[64,1,16]{2,1,0:T(1,128)S(1)}, u32[]{:S(2)}, u32[]{:S(2)}) %all-to-all-start.4) | async-done | bytes 4128 | tf_op jit(solution)/shard_map/all_to_all | solution.py:92
  252.8 1.9 gather_fusion
  (37 shorter events, 8.5 us)
Async XLA Ops:
  3.8 22.9 %all-to-all-start.1 = ((s32[64,1,16]{2,1,0:T(1,128)}), s32[64,1,16]{2,1,0:T(1,128)S(1)}, u32[]{:S(2)}, u32[]{:S(2)}) async-start(s32[64,1,16]{2,1,0:T(1,128)} %bitcast.7), calls=%async_computation.1 | async-start | bytes 65536 | tf_op jit(solution)/shard_map/all_to_all | solution.py:73
  26.6 13.9 %all-to-all-start = ((s32[64,1,16]{2,1,0:T(1,128)}), s32[64,1,16]{2,1,0:T(1,128)S(1)}, u32[]{:S(2)}, u32[]{:S(2)}) async-start(s32[64,1,16]{2,1,0:T(1,128)} %bitcast.6), calls=%async_computation | async-start | bytes 65536 | tf_op jit(solution)/shard_map/all_to_all | solution.py:72
  96.6 112.9 %all-to-all-start.3 = ((bf16[4,1024,1024]{2,1,0:T(8,128)(2,1)}), bf16[4,1024,1024]{2,1,0:T(8,128)(2,1)}, u32[]{:S(2)}, u32[]{:S(2)}) async-start(bf16[4,1024,1024]{2,1,0:T(8,128)(2,1)} %stack.3), calls=%async_computation.3 | async-start | bytes 16777216 | tf_op jit(solution)/shard_map/all_to_all | solution.py:85
  235.6 15.9 %all-to-all-start.4 = ((f32[64,1,16]{2,1,0:T(1,128)}), f32[64,1,16]{2,1,0:T(1,128)S(1)}, u32[]{:S(2)}, u32[]{:S(2)}) async-start(f32[64,1,16]{2,1,0:T(1,128)} %bitcast.12), calls=%async_computation.4 | async-start | bytes 65536 | tf_op jit(solution)/shard_map/all_to_all | solution.py:92
